TPU v7x, 32 devices: a whole 2x2x4 slice. The times are simulated.
32 devices in a mesh: dp: 4 (over y, x), tensor: 8 (over z, core).
Axes of the slice: x: 2, y: 2, z: 4, core: 2. Of those that a mesh axis runs over, the one named last changes fastest.
Arguments:
- tokens: bfloat16 [2048, 2048], P(('dp', 'tensor')), may hold values from -6 to 6
- cotangent: bfloat16 [2048, 2048], P(('dp', 'tensor')), may hold values from -6 to 6
- w_query: bfloat16 [2048, 2048], P(None, 'tensor'), may hold values from -0.125 to 0.125
- w_key: bfloat16 [2048, 2048], P(None, 'tensor'), may hold values from -0.125 to 0.125
- w_value: bfloat16 [2048, 2048], P(None, 'tensor'), may hold values from -0.125 to 0.125
- w_out: bfloat16 [2048, 2048], P('tensor'), may hold values from -0.125 to 0.125
- w_gate: bfloat16 [2048, 8192], P(None, 'tensor'), may hold values from -0.125 to 0.125
- w_up: bfloat16 [2048, 8192], P(None, 'tensor'), may hold values from -0.125 to 0.125
- w_down: bfloat16 [8192, 2048], P('tensor'), may hold values from -0.0625 to 0.0625
- q_gain: float32 [2048], P('tensor'), may hold values from 0.1 to 1.9
- k_gain: float32 [2048], P('tensor'), may hold values from 0.1 to 1.9
- attn_gain: float32 [2048], replicated, may hold values from 0.1 to 1.9
- ffn_gain: float32 [2048], replicated, may hold values from 0.1 to 1.9
Outputs:
- layer_out: float32 [2048, 2048], P(('dp', 'tensor'))
- grad_tokens: float32 [2048, 2048], P(('dp', 'tensor'))
- grad_w_query: float32 [2048, 2048], P(None, 'tensor')
- grad_w_key: float32 [2048, 2048], P(None, 'tensor')
- grad_w_value: float32 [2048, 2048], P(None, 'tensor')
- grad_w_out: float32 [2048, 2048], P('tensor')
- grad_w_gate: float32 [2048, 8192], P(None, 'tensor')
- grad_w_up: float32 [2048, 8192], P(None, 'tensor')
- grad_w_down: float32 [8192, 2048], P('tensor')
- grad_q_gain: float32 [2048], P('tensor')
- grad_k_gain: float32 [2048], P('tensor')
- grad_attn_gain: float32 [2048], replicated
- grad_ffn_gain: float32 [2048], replicated
All inputs are finite; a program needn't handle non-finite values.
Results may differ from a plain program's by a relative error of at most 0.015.
Values may be sent and summed in bfloat16 or wider, within the bound.
No kernel may reach another device: no remote copies, remote signals or barrier semaphores. Data moves between devices by JAX's collectives and lax.ppermute only.
A program may use at most 192 MiB of HBM per device.

v0:
```python
import math
import jax
import jax.numpy as jnp
from jax import lax
from jax.sharding import PartitionSpec as P

HD = 128
SEQ = 256
epsilon = 1e-06
rope_base = 500000.0


def rope_tables(length, head_width):
    half_width = head_width // 2
    exponent = jnp.arange(half_width, dtype=jnp.float32) * (2.0 / head_width)
    frequency = rope_base ** (-exponent)
    angles = jnp.arange(length, dtype=jnp.float32)[:, None] * frequency[None, :]
    cos_table = jnp.concatenate([jnp.cos(angles), jnp.cos(angles)], axis=1)
    sin_table = jnp.concatenate([jnp.sin(angles), jnp.sin(angles)], axis=1)
    return (cos_table[None, :, None, :], sin_table[None, :, None, :])


def rotate(field, cos_table, sin_table):
    half_width = field.shape[-1] // 2
    turned = jnp.concatenate([-field[..., half_width:], field[..., :half_width]], axis=-1)
    return field * cos_table + turned * sin_table


def unrotate(grad_field, cos_table, sin_table):
    half_width = grad_field.shape[-1] // 2
    moved = grad_field * sin_table
    back_part = jnp.concatenate([moved[..., half_width:], -moved[..., :half_width]], axis=-1)
    return grad_field * cos_table + back_part


def row_scale(matrix):
    return lax.rsqrt(jnp.mean(matrix * matrix, axis=1, keepdims=True) + epsilon)


def norm_back(grad_normed, normed, inverse):
    return inverse * (grad_normed - normed * jnp.mean(grad_normed * normed, axis=1, keepdims=True))


def product(left, right):
    return jnp.dot(left, right, preferred_element_type=jnp.float32)


def times_transposed(left, right):
    return lax.dot_general(
        left, right, (((1,), (1,)), ((), ())), preferred_element_type=jnp.float32
    )


def transposed_times(left, right):
    return lax.dot_general(
        left, right, (((0,), (0,)), ((), ())), preferred_element_type=jnp.float32
    )


def shards(
    tokens,
    cotangent,
    w_query,
    w_key,
    w_value,
    w_out,
    w_gate,
    w_up,
    w_down,
    q_gain,
    k_gain,
    attn_gain,
    ffn_gain,
):
    row_count = tokens.shape[0]
    model_width = tokens.shape[1]
    row_start = lax.axis_index("tensor") * row_count
    gathered = lax.all_gather(tokens, "tensor", axis=0, tiled=True)
    group_rows = gathered.shape[0]
    seq_count = group_rows // SEQ
    local_width = w_query.shape[1]
    local_heads = local_width // HD
    head_shape = (seq_count, SEQ, local_heads, HD)
    cos_table, sin_table = rope_tables(SEQ, HD)
    score_scale = 1.0 / math.sqrt(HD)
    query = product(gathered, w_query)
    keys = product(gathered, w_key)
    values = product(gathered, w_value).astype(jnp.bfloat16)
    q_squares, k_squares = lax.psum(
        (jnp.sum(query * query, axis=1), jnp.sum(keys * keys, axis=1)), "tensor"
    )
    q_inverse = lax.rsqrt(q_squares[:, None] / model_width + epsilon)
    k_inverse = lax.rsqrt(k_squares[:, None] / model_width + epsilon)
    q_normed = query * q_inverse
    k_normed = keys * k_inverse
    q_rot = rotate((q_normed * q_gain).reshape(head_shape), cos_table, sin_table).astype(
        jnp.bfloat16
    )
    k_rot = rotate((k_normed * k_gain).reshape(head_shape), cos_table, sin_table).astype(
        jnp.bfloat16
    )
    v_heads = values.reshape(head_shape)
    causal = jnp.arange(SEQ)[:, None] >= jnp.arange(SEQ)[None, :]
    scores = (
        jnp.einsum("sqhd,skhd->shqk", q_rot, k_rot, preferred_element_type=jnp.float32)
        * score_scale
    )
    scores = jnp.where(causal, scores, -1e30)
    top_score = jnp.max(scores, axis=3, keepdims=True)
    shifted = jnp.exp(scores - top_score)
    total = jnp.sum(shifted, axis=3, keepdims=True)
    probs = (shifted / total).astype(jnp.bfloat16)
    log_total = top_score + jnp.log(total)
    attended = jnp.einsum("shqk,skhd->sqhd", probs, v_heads, preferred_element_type=jnp.float32)
    attended = attended.astype(jnp.bfloat16).reshape(group_rows, local_width)
    attn_full = lax.psum(product(attended, w_out), "tensor")
    inverse_full = row_scale(attn_full)
    normed_full = attn_full * inverse_full
    mixed_full = gathered.astype(jnp.float32) + normed_full * attn_gain
    mixed_b = mixed_full.astype(jnp.bfloat16)
    a_inverse = lax.dynamic_slice_in_dim(inverse_full, row_start, row_count, 0)
    a_normed = lax.dynamic_slice_in_dim(normed_full, row_start, row_count, 0)
    mixed = lax.dynamic_slice_in_dim(mixed_full, row_start, row_count, 0)
    gate = product(mixed_b, w_gate)
    up_proj = product(mixed_b, w_up)
    sigmoid_gate = jax.nn.sigmoid(gate)
    activated = gate * sigmoid_gate
    swiglu = (activated * up_proj).astype(jnp.bfloat16)
    ffn_rows = lax.psum_scatter(product(swiglu, w_down), "tensor", scatter_dimension=0, tiled=True)
    m_inverse = row_scale(ffn_rows)
    m_normed = ffn_rows * m_inverse
    layer_out = mixed + m_normed * ffn_gain
    grad_out = cotangent.astype(jnp.float32)
    ffn_gain_part = jnp.sum(grad_out * m_normed, axis=0)
    grad_ffn = norm_back(grad_out * ffn_gain, m_normed, m_inverse).astype(jnp.bfloat16)
    grad_ffn_all = lax.all_gather(grad_ffn, "tensor", axis=0, tiled=True)
    grad_w_down = transposed_times(swiglu, grad_ffn_all)
    grad_swiglu = times_transposed(grad_ffn_all, w_down)
    grad_gate = (grad_swiglu * up_proj * sigmoid_gate * (1.0 + gate * (1.0 - sigmoid_gate))).astype(
        jnp.bfloat16
    )
    grad_up = (grad_swiglu * activated).astype(jnp.bfloat16)
    grad_w_gate = transposed_times(mixed_b, grad_gate)
    grad_w_up = transposed_times(mixed_b, grad_up)
    grad_mixed = grad_out + lax.psum_scatter(
        times_transposed(grad_gate, w_gate) + times_transposed(grad_up, w_up),
        "tensor",
        scatter_dimension=0,
        tiled=True,
    )
    attn_gain_part = jnp.sum(grad_mixed * a_normed, axis=0)
    grad_attn = norm_back(grad_mixed * attn_gain, a_normed, a_inverse).astype(jnp.bfloat16)
    grad_attn_all = lax.all_gather(grad_attn, "tensor", axis=0, tiled=True)
    grad_w_out = transposed_times(attended, grad_attn_all)
    grad_attended = times_transposed(grad_attn_all, w_out).astype(jnp.bfloat16)
    grad_heads = grad_attended.reshape(head_shape)
    prob_back = jnp.where(causal, jnp.exp(scores - log_total), 0.0)
    grad_values = jnp.einsum(
        "shqk,sqhd->skhd", probs, grad_heads, preferred_element_type=jnp.float32
    ).astype(jnp.bfloat16)
    grad_probs = jnp.einsum(
        "sqhd,skhd->shqk", grad_heads, v_heads, preferred_element_type=jnp.float32
    )
    inner = jnp.sum(prob_back * grad_probs, axis=3, keepdims=True)
    grad_scores = (prob_back * (grad_probs - inner) * score_scale).astype(jnp.bfloat16)
    grad_qrot = jnp.einsum(
        "shqk,skhd->sqhd", grad_scores, k_rot, preferred_element_type=jnp.float32
    )
    grad_krot = jnp.einsum(
        "shqk,sqhd->skhd", grad_scores, q_rot, preferred_element_type=jnp.float32
    )
    grad_qn = unrotate(grad_qrot, cos_table, sin_table).reshape(group_rows, local_width)
    grad_kn = unrotate(grad_krot, cos_table, sin_table).reshape(group_rows, local_width)
    grad_q_gain = jnp.sum(grad_qn * q_normed, axis=0)
    grad_k_gain = jnp.sum(grad_kn * k_normed, axis=0)
    q_target = grad_qn * q_gain
    k_target = grad_kn * k_gain
    q_inner, k_inner, grad_attn_gain, grad_ffn_gain = lax.psum(
        (
            jnp.sum(q_target * q_normed, axis=1),
            jnp.sum(k_target * k_normed, axis=1),
            attn_gain_part,
            ffn_gain_part,
        ),
        "tensor",
    )
    grad_query = (q_inverse * (q_target - q_normed * (q_inner[:, None] / model_width))).astype(
        jnp.bfloat16
    )
    grad_keys = (k_inverse * (k_target - k_normed * (k_inner[:, None] / model_width))).astype(
        jnp.bfloat16
    )
    grad_values = grad_values.reshape(group_rows, local_width)
    grad_w_query = transposed_times(gathered, grad_query)
    grad_w_key = transposed_times(gathered, grad_keys)
    grad_w_value = transposed_times(gathered, grad_values)
    grad_tokens = grad_mixed + lax.psum_scatter(
        times_transposed(grad_query, w_query)
        + times_transposed(grad_keys, w_key)
        + times_transposed(grad_values, w_value),
        "tensor",
        scatter_dimension=0,
        tiled=True,
    )
    (
        grad_w_query,
        grad_w_key,
        grad_w_value,
        grad_w_out,
        grad_w_gate,
        grad_w_up,
        grad_w_down,
        grad_q_gain,
        grad_k_gain,
        grad_attn_gain,
        grad_ffn_gain,
    ) = lax.psum(
        (
            grad_w_query,
            grad_w_key,
            grad_w_value,
            grad_w_out,
            grad_w_gate,
            grad_w_up,
            grad_w_down,
            grad_q_gain,
            grad_k_gain,
            grad_attn_gain,
            grad_ffn_gain,
        ),
        "dp",
    )
    return (
        layer_out,
        grad_tokens,
        grad_w_query,
        grad_w_key,
        grad_w_value,
        grad_w_out,
        grad_w_gate,
        grad_w_up,
        grad_w_down,
        grad_q_gain,
        grad_k_gain,
        grad_attn_gain,
        grad_ffn_gain,
    )


def solution(mesh):
    placed = (
        P(("dp", "tensor"), None),
        P(("dp", "tensor"), None),
        P(None, "tensor"),
        P(None, "tensor"),
        P(None, "tensor"),
        P("tensor", None),
        P(None, "tensor"),
        P(None, "tensor"),
        P("tensor", None),
        P("tensor"),
        P("tensor"),
        P(),
        P(),
    )
    return jax.shard_map(
        shards,
        mesh=mesh,
        in_specs=placed,
        out_specs=(
            P(("dp", "tensor"), None),
            P(("dp", "tensor"), None),
            P(None, "tensor"),
            P(None, "tensor"),
            P(None, "tensor"),
            P("tensor", None),
            P(None, "tensor"),
            P(None, "tensor"),
            P("tensor", None),
            P("tensor"),
            P("tensor"),
            P(),
            P(),
        ),
        check_vma=False,
    )
```

profile of v0, /device:TPU:0, one launch (start us, length us, event | category | flops | bytes accessed | tf_op | source)
XLA Modules:
  0.0 1108.2 jit_solution(12256830166530808767)
XLA Ops:
  9.6 31.9 %all-gather.4.cloned.1.call-done = bf16[512,2048]{1,0:T(8,128)(2,1)} async-done(((bf16[64,2048]{1,0:T(8,128)(2,1)}), bf16[512,2048]{1,0:T(8,128)(2,1)}) %all-gather.4.cloned.1.call-update) | async-done | bytes 2097168 | tf_op jit(solution)/shard_map/all_gather | solution.py:78
  41.5 3.4 convolution_convert_fusion.3
  44.9 1.0 reshape.124
  46.0 2.9 multiply_reduce_fusion.9
  48.8 1.6 multiply_reduce_fusion.10
  50.4 15.8 %all-reduce.1 = (f32[512]{0:T(512)S(1)}, f32[512]{0:T(512)}) all-reduce(f32[512]{0:T(512)S(1)} %get-tuple-element.87, f32[512]{0:T(512)S(1)} %get-tuple-element.89), channel_id=1, replica_groups=mesh['dp'=4,'tensor'=8] {'tensor'}, use_global_device_ids=true, to_apply=%region_1.0 | all-reduce | flops 1024 | bytes 8192 | tf_op jit(solution)/shard_map/psum | solution.py:89
  67.5 2.0 multiply_multiply_fusion
  69.4 2.2 reshape.126
  71.6 1.1 copy.50
  74.5 2.2 reshape.125
  76.7 1.2 copy.47
  82.1 1.1 copy.57
  83.3 4.0 fusion.42
  87.9 94.3 %all-reduce.7.cloned.1.call-done = f32[512,2048]{1,0:T(8,128)} async-done(((f32[512,2048]{1,0:T(8,128)}), f32[512,2048]{1,0:T(8,128)}) %all-reduce.7.cloned.1.call-update) | async-done | bytes 4194320 | tf_op jit(solution)/shard_map/psum | solution.py:116
  182.1 2.7 multiply_reduce_fusion
  185.6 4.7 fusion.60
  190.3 2.4 fusion.66
  193.3 3.7 multiply_convert_fusion.2
  198.0 4.4 fusion.67
  202.5 50.1 %reduce-scatter.4.cloned.1.call-done = f32[64,2048]{1,0:T(8,128)} async-done(((f32[512,2048]{1,0:T(8,128)}), f32[64,2048]{1,0:T(8,128)}) %reduce-scatter.4.cloned.1.call-update) | async-done | bytes 524304 | tf_op jit(solution)/shard_map/reduce_scatter | solution.py:129
  252.5 1.2 multiply_reduce_fusion.8
  253.7 1.8 fusion.19
  255.6 2.3 fusion.18
  258.1 27.6 %all-gather.6.cloned.1.call-done = bf16[512,2048]{1,0:T(8,128)(2,1)} async-done(((bf16[64,2048]{1,0:T(8,128)(2,1)}), bf16[512,2048]{1,0:T(8,128)(2,1)}) %all-gather.6.cloned.1.call-update) | async-done | bytes 2097168 | tf_op jit(solution)/shard_map/all_gather | solution.py:136
  285.7 7.1 multiply_convert_fusion
  292.8 2.4 fusion.68
  295.7 4.4 convolution_add_fusion
  300.2 1.3 dynamic-slice.3
  301.5 48.2 %reduce-scatter.6.cloned.1.call-done = f32[64,2048]{1,0:T(8,128)} async-done(((f32[512,2048]{1,0:T(8,128)}), f32[64,2048]{1,0:T(8,128)}) %reduce-scatter.6.cloned.1.call-update) | async-done | bytes 524304 | tf_op jit(solution)/shard_map/reduce_scatter | solution.py:145
  349.6 1.9 multiply_reduce_fusion.2
  351.6 2.1 multiply_convert_fusion.5
  353.7 27.7 %all-gather.8.cloned.1.call-done = bf16[512,2048]{1,0:T(8,128)(2,1)} async-done(((bf16[64,2048]{1,0:T(8,128)(2,1)}), bf16[512,2048]{1,0:T(8,128)(2,1)}) %all-gather.8.cloned.1.call-update) | async-done | bytes 2097168 | tf_op jit(solution)/shard_map/all_gather | solution.py:153
  381.4 3.3 convolution_convert_fusion.1
  384.7 1.7 reshape.128
  386.5 1.8 copy.64
  388.3 2.1 fusion.8
  390.4 2.3 fusion.49
  392.7 1.8 copy.66
  394.5 3.8 convolution_bitcast_fusion.4
  398.3 4.4 broadcast_multiply_fusion.1
  402.6 1.2 fusion.61
  403.8 1.1 fusion.62
  407.6 27.8 %all-reduce = (f32[512]{0:T(512)S(1)}, f32[512]{0:T(512)S(1)}, f32[2048]{0:T(1024)S(1)}, f32[2048]{0:T(1024)S(1)}) all-reduce(f32[512]{0:T(512)S(1)} %get-tuple-element.44, f32[512]{0:T(512)S(1)} %get-tuple-element.42, f32[2048]{0:T(1024)S(1)} %copy-done.44, f32[2048]{0:T(1024)S(1)} %copy-done.43), channel_id=1, replica_groups=mesh['dp'=4,'tensor'=8] {'tensor'}, use_global_device_ids=true, to_apply=%region_15.16 | all-reduce | flops 5120 | bytes 40960 | tf_op jit(solution)/shard_map/psum | solution.py:178
  435.4 1.3 multiply_convert_fusion.4
  436.8 1.4 multiply_convert_fusion.3
  440.8 2.8 add_add_fusion
  443.7 7.8 fusion.72
  451.6 5.8 fusion.71
  457.4 5.8 fusion.73
  463.2 2.1 fusion.40
  465.2 2.0 convolution_bitcast_fusion.1
  467.3 2.0 convolution_bitcast_fusion.2
  469.3 2.1 convolution_bitcast_fusion
  471.4 16.9 %all-reduce.2 = (f32[256]{0:T(256)}, f32[256]{0:T(256)}, f32[2048]{0:T(1024)}, f32[2048]{0:T(1024)}) all-reduce(f32[256]{0:T(256)S(1)} %get-tuple-element.43, f32[256]{0:T(256)S(1)} %get-tuple-element.41, f32[2048]{0:T(1024)S(1)} %get-tuple-element.49, f32[2048]{0:T(1024)S(1)} %get-tuple-element.50), channel_id=1, replica_groups=mesh['dp'=4,'tensor'=8] {'dp'}, use_global_device_ids=true, to_apply=%region_27.28 | all-reduce | flops 4608 | bytes 36864 | tf_op jit(solution)/shard_map/psum | solution.py:217
  488.3 3.6 reduce-scatter.8.cloned.1.call-done
  491.9 1.9 fusion.53
  493.8 580.4 %all-reduce.9.cloned.1.call-done = (f32[2048,256]{0,1:T(8,128)}, f32[2048,256]{0,1:T(8,128)}, f32[2048,256]{0,1:T(8,128)}, f32[256,2048]{1,0:T(8,128)}, f32[2048...) async-done(((f32[2048,256]{0,1:T(8,128)}, f32[2048,256]{0,1:T(8,128)}, f32[2048,256]{0,1:T(8,128)}, f32[256,2048]{1,0:T(8,128)}, f32[2048,1024]{1,0:T(8,128)}, ...) | async-done | bytes 33554448 | tf_op jit(solution)/shard_map/psum | solution.py:217
  1074.2 3.0 copy.67
  1077.2 1.8 copy.68
  1079.0 3.0 copy.69
  1082.1 1.3 copy.110
  1083.4 9.1 copy.111
  1092.6 4.3 copy.112
  1097.8 3.4 copy.113
  (179 shorter events, 19.7 us)
Async XLA Ops:
  7.2 41.7 %copy-start = (bf16[2048,256]{1,0:T(8,128)(2,1)S(1)}, bf16[2048,256]{1,0:T(8,128)(2,1)}, u32[]{:S(2)}) copy-start(bf16[2048,256]{1,0:T(8,128)(2,1)} %param.15) | copy-start | bytes 3145732
  7.2 34.3 %all-gather.4.cloned.1.call-start = ((), (), s32[]{:S(2)}) async-start(), calls=%async_computation.3 | async-start | bytes 2359296 | tf_op jit(solution)/shard_map/all_gather | solution.py:78
  7.9 174.2 %all-reduce.7.cloned.1.call-start = ((), (), s32[]{:S(2)}) async-start(), calls=%async_computation.4 | async-start | bytes 8388608 | tf_op jit(solution)/shard_map/psum | solution.py:116
  41.5 4.4 copy-start.2
  46.0 34.4 %copy-start.22 = (bf16[2,256,2,128]{3,2,1,0:T(2,128)(2,1)}, bf16[2,256,2,128]{3,2,1,0:T(2,128)(2,1)S(1)}, u32[]{:S(2)}) copy-start(bf16[2,256,2,128]{3,2,1,0:T(2,128)(2,1)S(1)} %reshape.124) | copy-start | bytes 786436
  48.8 18.6 %copy-start.47 = (f32[256]{0:T(256)S(1)}, f32[256]{0:T(256)}, u32[]{:S(2)}) copy-start(f32[256]{0:T(256)} %param.23) | copy-start | bytes 3076
  66.9 6.6 copy-start.41
  67.5 6.1 copy-start.45
  71.6 2.0 copy-start.8
  76.6 1.3 copy-start.13
  76.6 1.4 copy-start.14
  76.7 1.4 copy-start.30
  76.7 1.5 copy-start.31
  76.7 1.5 copy-start.36
  78.4 1.9 copy-start.28
  78.4 1.9 copy-start.29
  83.2 4.1 copy-start.15
  87.3 97.5 %copy-start.38 = (f32[2048]{0:T(1024)S(1)}, f32[2048]{0:T(1024)}, u32[]{:S(2)}) copy-start(f32[2048]{0:T(1024)} %param.24) | copy-start | bytes 24580
  87.3 165.2 %reduce-scatter.4.cloned.1.call-start = ((), (), s32[]{:S(2)}) async-start(), calls=%async_computation.5 | async-start | bytes 4718592 | tf_op jit(solution)/shard_map/reduce_scatter | solution.py:129
  182.1 3.4 copy-start.3
  185.6 4.7 copy-start.49
  185.6 4.8 copy-start.51
  190.3 2.4 copy-start.26
  190.3 2.9 copy-start.53
  193.3 3.7 copy-start.61
  193.3 4.7 copy-start.50
  202.4 51.3 %copy-start.5 = (bf16[64,2048]{1,0:T(8,128)(2,1)S(1)}, bf16[64,2048]{1,0:T(8,128)(2,1)}, u32[]{:S(2)}) copy-start(bf16[64,2048]{1,0:T(8,128)(2,1)} %param.14) | copy-start | bytes 786436
  202.4 83.2 %all-gather.6.cloned.1.call-start = ((), (), s32[]{:S(2)}) async-start(), calls=%async_computation.6 | async-start | bytes 2359296 | tf_op jit(solution)/shard_map/all_gather | solution.py:136
  257.9 91.8 %reduce-scatter.6.cloned.1.call-start = ((), (), s32[]{:S(2)}) async-start(), calls=%async_computation.7 | async-start | bytes 4718592 | tf_op jit(solution)/shard_map/reduce_scatter | solution.py:145
  285.7 7.1 copy-start.52
  292.8 2.4 copy-start.56
  292.8 2.4 copy-start.58
  292.8 2.9 copy-start.54
  300.2 81.3 %all-gather.8.cloned.1.call-start = ((), (), s32[]{:S(2)}) async-start(), calls=%async_computation.8 | async-start | bytes 2359296 | tf_op jit(solution)/shard_map/all_gather | solution.py:153
  353.7 138.2 %reduce-scatter.8.cloned.1.call-start = ((), (), s32[]{:S(2)}) async-start(), calls=%async_computation.9 | async-start | bytes 4718592 | tf_op jit(solution)/shard_map/reduce_scatter | solution.py:197
  402.6 2.2 copy-start.34
  402.6 2.3 copy-start.35
  404.9 1.0 copy-start.7
  404.9 1.0 copy-start.40
  405.5 1.3 copy-start.9
  405.5 1.3 copy-start.42
  405.5 1.3 copy-start.46
  405.9 1.7 copy-start.43
  405.9 1.7 copy-start.44
  436.7 2.2 copy-start.17
  438.2 1.3 copy-start.32
  439.5 1.3 copy-start.33
  443.7 630.5 %all-reduce.9.cloned.1.call-start = ((), (), s32[]{:S(2)}) async-start(), calls=%async_computation.10 | async-start | bytes 67108864 | tf_op jit(solution)/shard_map/psum | solution.py:217
  443.7 7.8 copy-start.27
  443.7 7.8 copy-start.57
  451.5 5.8 copy-start.55
  451.5 5.8 copy-start.60
  457.4 5.8 copy-start.16
  457.4 5.8 copy-start.23
  463.2 2.1 copy-start.20
  465.2 2.0 copy-start.18
  471.4 20.5 %copy-start.6 = (f32[64,2048]{1,0:T(8,128)S(1)}, f32[64,2048]{1,0:T(8,128)}, u32[]{:S(2)}) copy-start(f32[64,2048]{1,0:T(8,128)} %reduce-scatter.6.cloned.1.call-done) | copy-start | bytes 1572868
  1074.2 3.0 copy-start.25
  1079.0 3.0 copy-start.24
  1082.1 10.5 slice-start.2
  1083.4 9.1 slice-start.3
  1083.4 13.4 %slice-start = ((s8[8388608]{0:T(1024)(128)(4,1)}), s8[4194304]{0:T(1024)(128)(4,1)S(1)}, s32[]{:S(2)}) async-start(s8[8388608]{0:T(1024)(128)(4,1)} %bitcast.88), calls=%async_computation.11 | async-start | bytes 8388608
  1092.6 5.2 slice-start.1
  1097.8 3.4 copy-start.1
  (10 other events, 8.6 us)
Sparse Core Ops, SparseCore 0:
  9.6 31.8 all-gather.3
  87.5 94.6 all-reduce.6
  202.5 49.9 reduce-scatter.3
  258.0 27.6 all-gather.5
  300.3 49.3 reduce-scatter.5
  353.8 27.6 all-gather.7
  443.8 48.0 reduce-scatter.7
  497.8 576.3 all-reduce.8
where the time goes:
time: 1110 us
  waiting for transfers between devices  864 us (78%)
  matrix products  85.4 us (8%)
  blocking collectives  60.5 us (5%)
  local copies, waits for them, and re-layouts  51.2 us (5%)
  other arithmetic  30.8 us (3%)
  between operations  15 us (1%)
    psum x1, waiting for transfers between devices, shards(): lax.psum((grad_w_query, grad_w_key, grad_w_value, grad_w_out, grad_w_gate...  580 us
    psum x1, waiting for transfers between devices, shards(): attn_full = lax.psum(product(attended, w_out), 'tensor')  94.3 us
    reduce_scatter x1, waiting for transfers between devices, shards(): lax.psum_scatter(product(swiglu, w_down), 'tensor', scatter_dimension=0,...  50.1 us
    reduce_scatter x1, waiting for transfers between devices, shards(): lax.psum_scatter(times_transposed(grad_gate, w_gate) + times_transposed(g...  48.2 us
    unnamed x141, local copies, waits for them, and re-layouts  35 us
    all_gather x1, waiting for transfers between devices, shards(): gathered = lax.all_gather(tokens, 'tensor', axis=0, tiled=True)  31.9 us
    psum x1, blocking collectives, shards(): lax.psum((jnp.sum(q_target * q_normed, axis=1), jnp.sum(k_target * k_norm...  27.8 us
    all_gather x1, waiting for transfers between devices, shards(): grad_attn_all = lax.all_gather(grad_attn, 'tensor', axis=0, tiled=True)  27.7 us
  transfers between devices with their start and end apart: 8, of which 8 were waited for; matrix products, arithmetic and copies ran while one was open for 3% of the time, Pallas kernels for 0%

commit v1 on v0

--- a/solution.py
+++ b/solution.py
@@ -113,7 +113,9 @@
     log_total = top_score + jnp.log(total)
     attended = jnp.einsum("shqk,skhd->sqhd", probs, v_heads, preferred_element_type=jnp.float32)
     attended = attended.astype(jnp.bfloat16).reshape(group_rows, local_width)
-    attn_full = lax.psum(product(attended, w_out), "tensor")
+    x = product(attended, w_out)
+    blocks = lax.all_gather(x, "tensor", axis=0, tiled=False)
+    attn_full = blocks.sum(axis=0)
     inverse_full = row_scale(attn_full)
     normed_full = attn_full * inverse_full
     mixed_full = gathered.astype(jnp.float32) + normed_full * attn_gain

time: 1110 us -> 1320 us (1.19)
  waiting for transfers between devices: 864 us -> 1050 us
  other arithmetic: 30.8 us -> 44.9 us
    all_gather x0 -> x1, waiting for transfers between devices: none -> 286 us  [shards(): blocks = lax.all_gather(x, 'tensor', axis=0, tiled=False)]
    psum x1 -> x0, waiting for transfers between devices: 94.3 us -> none  [shards(): attn_full = lax.psum(product(attended, w_out), 'tensor')]
    reduce_sum x0 -> x1, other arithmetic: none -> 14.1 us  [shards(): attn_full = blocks.sum(axis=0)]
  transfers between devices with their start and end apart: 8 -> 8, of which waited for: 8 -> 8; matrix products, arithmetic and copies ran while one was open for 3% -> 2% of each run, Pallas kernels for 0% -> 0%
where the time goes in v1:
time: 1320 us; the launch traced here: 1310 us
  waiting for transfers between devices  1050 us (80%)
  matrix products  85.4 us (6%)
  blocking collectives  60.5 us (5%)
  local copies, waits for them, and re-layouts  51.2 us (4%)
  other arithmetic  44.9 us (3%)
  between operations  15 us (1%)
    psum x1, waiting for transfers between devices, shards(): lax.psum((grad_w_query, grad_w_key, grad_w_value, grad_w_out, grad_w_gate...  580 us
    all_gather x1, waiting for transfers between devices, shards(): blocks = lax.all_gather(x, 'tensor', axis=0, tiled=False)  286 us
    reduce_scatter x1, waiting for transfers between devices, shards(): lax.psum_scatter(product(swiglu, w_down), 'tensor', scatter_dimension=0,...  48.2 us
    reduce_scatter x1, waiting for transfers between devices, shards(): lax.psum_scatter(times_transposed(grad_gate, w_gate) + times_transposed(g...  48.2 us
    unnamed x141, local copies, waits for them, and re-layouts  35 us
    all_gather x1, waiting for transfers between devices, shards(): gathered = lax.all_gather(tokens, 'tensor', axis=0, tiled=True)  31.9 us
    psum x1, blocking collectives, shards(): lax.psum((jnp.sum(q_target * q_normed, axis=1), jnp.sum(k_target * k_norm...  27.8 us
    all_gather x1, waiting for transfers between devices, shards(): grad_attn_all = lax.all_gather(grad_attn, 'tensor', axis=0, tiled=True)  27.7 us
  transfers between devices with their start and end apart: 8, of which 8 were waited for; matrix products, arithmetic and copies ran while one was open for 2% of the time, Pallas kernels for 0%

profile of v1, /device:TPU:0, one launch (start us, length us, event | category | flops | bytes accessed | tf_op | source)
XLA Modules:
  0.0 1312.7 jit_solution(12331498837870572952)
XLA Ops:
  9.6 31.9 %all-gather.6.cloned.1.call-done = bf16[512,2048]{1,0:T(8,128)(2,1)} async-done(((bf16[64,2048]{1,0:T(8,128)(2,1)}), bf16[512,2048]{1,0:T(8,128)(2,1)}) %all-gather.6.cloned.1.call-update) | async-done | bytes 2097168 | tf_op jit(solution)/shard_map/all_gather | solution.py:78
  41.5 3.4 convolution_convert_fusion.3
  46.0 2.9 multiply_reduce_fusion.9
  48.8 1.6 multiply_reduce_fusion.10
  50.4 15.8 %all-reduce.1 = (f32[512]{0:T(512)S(1)}, f32[512]{0:T(512)}) all-reduce(f32[512]{0:T(512)S(1)} %get-tuple-element.87, f32[512]{0:T(512)S(1)} %get-tuple-element.89), channel_id=1, replica_groups=mesh['dp'=4,'tensor'=8] {'tensor'}, use_global_device_ids=true, to_apply=%region_1.0 | all-reduce | flops 1024 | bytes 8192 | tf_op jit(solution)/shard_map/psum | solution.py:89
  67.5 2.0 multiply_multiply_fusion
  69.4 2.2 reshape.126
  71.6 1.1 copy.50
  74.5 2.2 reshape.125
  76.7 1.2 copy.47
  82.1 1.1 copy.57
  83.3 4.0 fusion.42
  87.9 286.4 %all-gather.12.cloned.1.call-done = f32[4096,2048]{1,0:T(8,128)} async-done(((f32[512,2048]{1,0:T(8,128)}), f32[4096,2048]{1,0:T(8,128)}) %all-gather.12.cloned.1.call-update) | async-done | bytes 33554448 | tf_op jit(solution)/shard_map/all_gather | solution.py:117
  374.2 14.1 %reduce_sum.138 = f32[512,2048]{1,0:T(8,128)} reduce(f32[8,512,2048]{2,1,0:T(8,128)} %bitcast.89, f32[]{:T(128)} %constant.13.clone.1), dimensions={0}, to_apply=%region_6.7 | reduce | flops 7340032 | bytes 37748740 | tf_op jit(solution)/shard_map/reduce_sum | solution.py:118
  388.4 2.7 multiply_reduce_fusion
  391.8 4.7 fusion.60
  396.6 2.4 fusion.66
  399.5 3.7 multiply_convert_fusion.2
  404.3 4.4 fusion.67
  408.7 48.2 %reduce-scatter.4.cloned.1.call-done = f32[64,2048]{1,0:T(8,128)} async-done(((f32[512,2048]{1,0:T(8,128)}), f32[64,2048]{1,0:T(8,128)}) %reduce-scatter.4.cloned.1.call-update) | async-done | bytes 524304 | tf_op jit(solution)/shard_map/reduce_scatter | solution.py:131
  456.9 1.2 multiply_reduce_fusion.8
  458.1 1.8 fusion.19
  460.0 2.3 fusion.18
  462.5 27.6 %all-gather.8.cloned.1.call-done = bf16[512,2048]{1,0:T(8,128)(2,1)} async-done(((bf16[64,2048]{1,0:T(8,128)(2,1)}), bf16[512,2048]{1,0:T(8,128)(2,1)}) %all-gather.8.cloned.1.call-update) | async-done | bytes 2097168 | tf_op jit(solution)/shard_map/all_gather | solution.py:138
  490.1 7.1 multiply_convert_fusion
  497.2 2.4 fusion.68
  500.2 4.4 convolution_add_fusion
  504.6 1.3 dynamic-slice.3
  505.9 48.2 %reduce-scatter.6.cloned.1.call-done = f32[64,2048]{1,0:T(8,128)} async-done(((f32[512,2048]{1,0:T(8,128)}), f32[64,2048]{1,0:T(8,128)}) %reduce-scatter.6.cloned.1.call-update) | async-done | bytes 524304 | tf_op jit(solution)/shard_map/reduce_scatter | solution.py:147
  554.0 1.9 multiply_reduce_fusion.2
  556.0 2.1 multiply_convert_fusion.5
  558.1 27.7 %all-gather.10.cloned.1.call-done = bf16[512,2048]{1,0:T(8,128)(2,1)} async-done(((bf16[64,2048]{1,0:T(8,128)(2,1)}), bf16[512,2048]{1,0:T(8,128)(2,1)}) %all-gather.10.cloned.1.call-update) | async-done | bytes 2097168 | tf_op jit(solution)/shard_map/all_gather | solution.py:155
  585.8 3.3 convolution_convert_fusion.1
  589.1 1.7 reshape.128
  590.9 1.8 copy.64
  592.7 2.1 fusion.8
  594.8 2.3 fusion.49
  597.1 1.8 copy.66
  598.9 3.8 convolution_bitcast_fusion.4
  602.7 4.4 broadcast_multiply_fusion.1
  607.0 1.2 fusion.61
  608.2 1.1 fusion.62
  612.0 27.8 %all-reduce = (f32[512]{0:T(512)S(1)}, f32[512]{0:T(512)S(1)}, f32[2048]{0:T(1024)S(1)}, f32[2048]{0:T(1024)S(1)}) all-reduce(f32[512]{0:T(512)S(1)} %get-tuple-element.44, f32[512]{0:T(512)S(1)} %get-tuple-element.42, f32[2048]{0:T(1024)S(1)} %copy-done.44, f32[2048]{0:T(1024)S(1)} %copy-done.43), channel_id=1, replica_groups=mesh['dp'=4,'tensor'=8] {'tensor'}, use_global_device_ids=true, to_apply=%region_15.16 | all-reduce | flops 5120 | bytes 40960 | tf_op jit(solution)/shard_map/psum | solution.py:180
  639.8 1.3 multiply_convert_fusion.4
  641.2 1.4 multiply_convert_fusion.3
  645.3 2.8 add_add_fusion
  648.2 7.8 fusion.72
  656.0 5.8 fusion.71
  661.8 5.8 fusion.73
  667.6 2.1 fusion.40
  669.7 2.0 convolution_bitcast_fusion.1
  671.7 2.0 convolution_bitcast_fusion.2
  673.7 2.1 convolution_bitcast_fusion
  675.8 16.9 %all-reduce.2 = (f32[256]{0:T(256)}, f32[256]{0:T(256)}, f32[2048]{0:T(1024)}, f32[2048]{0:T(1024)}) all-reduce(f32[256]{0:T(256)S(1)} %get-tuple-element.43, f32[256]{0:T(256)S(1)} %get-tuple-element.41, f32[2048]{0:T(1024)S(1)} %get-tuple-element.49, f32[2048]{0:T(1024)S(1)} %get-tuple-element.50), channel_id=1, replica_groups=mesh['dp'=4,'tensor'=8] {'dp'}, use_global_device_ids=true, to_apply=%region_27.28 | all-reduce | flops 4608 | bytes 36864 | tf_op jit(solution)/shard_map/psum | solution.py:219
  692.7 3.6 reduce-scatter.8.cloned.1.call-done
  696.3 1.9 fusion.53
  698.2 580.4 %all-reduce.6.cloned.1.call-done = (f32[2048,256]{0,1:T(8,128)}, f32[2048,256]{0,1:T(8,128)}, f32[2048,256]{0,1:T(8,128)}, f32[256,2048]{1,0:T(8,128)}, f32[2048...) async-done(((f32[2048,256]{0,1:T(8,128)}, f32[2048,256]{0,1:T(8,128)}, f32[2048,256]{0,1:T(8,128)}, f32[256,2048]{1,0:T(8,128)}, f32[2048,1024]{1,0:T(8,128)}, ...) | async-done | bytes 33554448 | tf_op jit(solution)/shard_map/psum | solution.py:219
  1278.6 3.0 copy.67
  1281.7 1.8 copy.68
  1283.5 3.0 copy.69
  1286.5 1.3 copy.109
  1287.8 9.1 copy.110
  1297.0 4.3 copy.111
  1302.2 3.4 copy.112
  (180 shorter events, 20.7 us)
Async XLA Ops:
  7.2 41.7 %copy-start = (bf16[2048,256]{1,0:T(8,128)(2,1)S(1)}, bf16[2048,256]{1,0:T(8,128)(2,1)}, u32[]{:S(2)}) copy-start(bf16[2048,256]{1,0:T(8,128)(2,1)} %param.15) | copy-start | bytes 3145732
  7.2 34.3 %all-gather.6.cloned.1.call-start = ((), (), s32[]{:S(2)}) async-start(), calls=%async_computation.3 | async-start | bytes 2359296 | tf_op jit(solution)/shard_map/all_gather | solution.py:78
  7.9 366.3 %all-gather.12.cloned.1.call-start = ((), (), s32[]{:S(2)}) async-start(), calls=%async_computation.9 | async-start | bytes 37748736 | tf_op jit(solution)/shard_map/all_gather | solution.py:117
  41.5 4.4 copy-start.3
  46.0 34.4 %copy-start.22 = (bf16[2,256,2,128]{3,2,1,0:T(2,128)(2,1)}, bf16[2,256,2,128]{3,2,1,0:T(2,128)(2,1)S(1)}, u32[]{:S(2)}) copy-start(bf16[2,256,2,128]{3,2,1,0:T(2,128)(2,1)S(1)} %reshape.124) | copy-start | bytes 786436
  48.8 18.6 %copy-start.47 = (f32[256]{0:T(256)S(1)}, f32[256]{0:T(256)}, u32[]{:S(2)}) copy-start(f32[256]{0:T(256)} %param.23) | copy-start | bytes 3076
  66.9 6.6 copy-start.41
  67.5 6.1 copy-start.45
  71.6 2.0 copy-start.8
  76.6 1.3 copy-start.13
  76.6 1.4 copy-start.14
  76.6 1.4 copy-start.30
  76.6 1.5 copy-start.31
  76.6 1.5 copy-start.36
  78.4 1.9 copy-start.28
  78.4 1.9 copy-start.29
  83.2 4.1 copy-start.15
  87.3 369.6 %reduce-scatter.4.cloned.1.call-start = ((), (), s32[]{:S(2)}) async-start(), calls=%async_computation.4 | async-start | bytes 4718592 | tf_op jit(solution)/shard_map/reduce_scatter | solution.py:131
  374.2 16.8 %copy-start.38 = (f32[2048]{0:T(1024)S(1)}, f32[2048]{0:T(1024)}, u32[]{:S(2)}) copy-start(f32[2048]{0:T(1024)} %param.24) | copy-start | bytes 24580
  388.4 3.4 copy-start.2
  391.8 4.7 copy-start.49
  391.8 4.8 copy-start.51
  396.6 2.4 copy-start.26
  396.6 2.9 copy-start.53
  399.5 3.7 copy-start.61
  399.5 4.7 copy-start.50
  408.6 49.5 %copy-start.5 = (bf16[64,2048]{1,0:T(8,128)(2,1)S(1)}, bf16[64,2048]{1,0:T(8,128)(2,1)}, u32[]{:S(2)}) copy-start(bf16[64,2048]{1,0:T(8,128)(2,1)} %param.14) | copy-start | bytes 786436
  408.7 81.4 %all-gather.8.cloned.1.call-start = ((), (), s32[]{:S(2)}) async-start(), calls=%async_computation.5 | async-start | bytes 2359296 | tf_op jit(solution)/shard_map/all_gather | solution.py:138
  462.3 91.8 %reduce-scatter.6.cloned.1.call-start = ((), (), s32[]{:S(2)}) async-start(), calls=%async_computation.6 | async-start | bytes 4718592 | tf_op jit(solution)/shard_map/reduce_scatter | solution.py:147
  490.1 7.1 copy-start.52
  497.2 2.4 copy-start.56
  497.2 2.4 copy-start.58
  497.2 2.9 copy-start.54
  504.6 81.3 %all-gather.10.cloned.1.call-start = ((), (), s32[]{:S(2)}) async-start(), calls=%async_computation.7 | async-start | bytes 2359296 | tf_op jit(solution)/shard_map/all_gather | solution.py:155
  558.1 138.3 %reduce-scatter.8.cloned.1.call-start = ((), (), s32[]{:S(2)}) async-start(), calls=%async_computation.8 | async-start | bytes 4718592 | tf_op jit(solution)/shard_map/reduce_scatter | solution.py:199
  607.0 2.2 copy-start.34
  607.0 2.3 copy-start.35
  609.3 1.0 copy-start.7
  609.3 1.0 copy-start.40
  609.9 1.3 copy-start.9
  609.9 1.3 copy-start.42
  609.9 1.3 copy-start.46
  610.4 1.7 copy-start.43
  610.4 1.7 copy-start.44
  641.2 2.2 copy-start.17
  642.6 1.3 copy-start.32
  644.0 1.3 copy-start.33
  648.1 630.5 %all-reduce.6.cloned.1.call-start = ((), (), s32[]{:S(2)}) async-start(), calls=%async_computation.10 | async-start | bytes 67108864 | tf_op jit(solution)/shard_map/psum | solution.py:219
  648.2 7.8 copy-start.27
  648.2 7.8 copy-start.57
  656.0 5.8 copy-start.55
  656.0 5.8 copy-start.60
  661.8 5.8 copy-start.16
  661.8 5.8 copy-start.23
  667.6 2.1 copy-start.20
  669.7 2.0 copy-start.18
  675.8 20.5 %copy-start.6 = (f32[64,2048]{1,0:T(8,128)S(1)}, f32[64,2048]{1,0:T(8,128)}, u32[]{:S(2)}) copy-start(f32[64,2048]{1,0:T(8,128)} %reduce-scatter.6.cloned.1.call-done) | copy-start | bytes 1572868
  1278.6 3.0 copy-start.25
  1283.5 3.0 copy-start.24
  1286.5 10.5 slice-start.2
  1287.8 9.1 slice-start.3
  1287.8 13.4 %slice-start = ((s8[8388608]{0:T(1024)(128)(4,1)}), s8[4194304]{0:T(1024)(128)(4,1)S(1)}, s32[]{:S(2)}) async-start(s8[8388608]{0:T(1024)(128)(4,1)} %bitcast.90), calls=%async_computation.11 | async-start | bytes 8388608
  1297.0 5.2 slice-start.1
  1302.2 3.4 copy-start.1
  (10 other events, 8.6 us)
Sparse Core Ops, SparseCore 0:
  9.6 31.8 all-gather.5
  87.5 286.7 all-gather.11
  408.8 48.0 reduce-scatter.3
  462.4 27.6 all-gather.7
  504.7 49.3 reduce-scatter.5
  558.2 27.6 all-gather.9
  648.2 48.0 reduce-scatter.7
  702.2 576.3 all-reduce.5
